TPU v7x, 32 devices: a whole 2x2x4 slice. The times are simulated.
32 devices in a mesh: row: 8 (over y, x, core), col: 4 (over z).
Axes of the slice: x: 2, y: 2, z: 4, core: 2. Of those that a mesh axis runs over, the one named last changes fastest.
Arguments:
- row_geometry: float32 [4, 8, 16, 4, 2, 256], P('col', 'row'), may hold values from 0 to 1, as said below
- column_geometry: float32 [4, 2, 512], replicated, may hold values from 0 to 1
- octree_slot: int32 [4, 8, 8, 2], P('col'), may hold values from 0 to 15, as said below
- pivots: int32 [256], replicated, may hold values from 0 to 65535, as said below
- lower_inv: float32 [256, 256], replicated, as said below
- upper_inv: float32 [256, 256], replicated, as said below
Outputs:
- slab_out: float32 [8, 4, 8, 256, 512], P('row', 'col')
- upper_block: float32 [256, 256], replicated
Inputs may be any that keep to these rules, and one draw needn't show every extreme that they name: For each process column q and owner d, the entries octree_slot[q, :, d, :] are each local tile number 0 to 15 once. pivots[i] lies between i and 65535. `row_geometry`: the two tiles of one tile row carry equal row geometry in their slots. `lower_inv`: unit lower triangular. `upper_inv`: upper triangular with positive diagonal.
All inputs are finite; a program needn't handle non-finite values.
Results may differ from a plain program's by a relative error of at most 0.0003.
Values sent between devices are 32-bit elements; how exact they have to be, the bound alone decides.
No kernel may reach another device: no remote copies, remote signals or barrier semaphores. Data moves between devices by JAX's collectives and lax.ppermute only.
A program may use at most 64 MiB of HBM per device.

v0:
```python
import jax
import jax.numpy as jnp
from jax import lax
from jax.sharding import PartitionSpec as P

KAPPA = 9.0
SOFTEN = 0.05


def kernel_entries(row_points, column_points):
    quad_count = row_points.shape[-2]
    accumulated = None
    for row_point in range(quad_count):
        for column_point in range(quad_count):
            along_x = (
                row_points[..., 0, row_point, :, None]
                - column_points[..., 0, column_point, None, :]
            )
            along_y = (
                row_points[..., 1, row_point, :, None]
                - column_points[..., 1, column_point, None, :]
            )
            along_z = (
                row_points[..., 2, row_point, :, None]
                - column_points[..., 2, column_point, None, :]
            )
            spacing = jnp.sqrt(along_x * along_x + along_y * along_y + along_z * along_z)
            summand = (
                row_points[..., 3, row_point, :, None]
                * column_points[..., 3, column_point, None, :]
                * jnp.cos(KAPPA * spacing)
                / (spacing + SOFTEN)
            )
            accumulated = summand if accumulated is None else accumulated + summand
    return accumulated


def tracked_swaps(pivots):
    tile_size = pivots.shape[0]
    positions = jnp.concatenate([jnp.arange(tile_size, dtype=jnp.int32), pivots])
    same = positions[:, None] == positions[None, :]
    first_slot = jnp.argmax(same, axis=1)

    def advance(index_now, compact):
        slot_here = first_slot[index_now]
        slot_there = first_slot[index_now + tile_size]
        at_step = compact[slot_here]
        at_target = compact[slot_there]
        return compact.at[slot_here].set(at_target).at[slot_there].set(at_step)

    compact = lax.fori_loop(0, tile_size, advance, positions)
    values = jnp.take(compact, first_slot, axis=0)
    return (positions, values)


def per_device(row_geometry, column_geometry, octree_slot, pivots, lower_inv, upper_inv):
    row_count = lax.axis_size("row")
    col_count = lax.axis_size("col")
    row_place = lax.axis_index("row")
    col_place = lax.axis_index("col")
    tile_size = pivots.shape[0]
    slots_all = row_geometry.shape[2]
    tile_rows_dev = slots_all // 2
    quad_count = row_geometry.shape[4]
    fill_geometry = row_geometry[0, 0]
    slot_table = octree_slot[0]
    fill_tiles = lax.dynamic_index_in_dim(slot_table, row_place, 0, keepdims=False).reshape(-1)
    arrival = lax.dynamic_index_in_dim(slot_table, row_place, 1, keepdims=False).reshape(-1)
    placement_index = (
        jnp.zeros((slots_all,), jnp.int32).at[arrival].set(jnp.arange(slots_all, dtype=jnp.int32))
    )
    column_halves = column_geometry.reshape(4, quad_count, 2, tile_size)
    halves = jnp.take(column_halves, fill_tiles % 2, axis=2)
    filled = kernel_entries(fill_geometry, jnp.transpose(halves, (2, 0, 1, 3)))
    arrived = lax.all_to_all(filled, "row", split_axis=0, concat_axis=0, tiled=True)
    owned_tiles = jnp.take(arrived, placement_index, axis=0)
    slab_rows = (
        owned_tiles.reshape(tile_rows_dev, 2, tile_size, tile_size)
        .transpose(0, 2, 1, 3)
        .reshape(tile_rows_dev * tile_size, 2 * tile_size)
    )
    positions, values = tracked_swaps(pivots)
    local_tile_rows = row_place + row_count * (
        col_place + col_count * jnp.arange(tile_rows_dev, dtype=jnp.int32)
    )
    global_rows = (
        local_tile_rows[:, None] * tile_size + jnp.arange(tile_size, dtype=jnp.int32)[None, :]
    ).reshape(-1)
    matched = global_rows[:, None] == positions[None, :]
    found = jnp.max(jnp.where(matched, values[None, :], -1), axis=1)
    sources = jnp.where(found >= 0, found, global_rows)
    pivot_sources = values[:tile_size]
    source_tiles = pivot_sources // tile_size
    holds_row = (source_tiles % row_count == row_place) & (
        source_tiles // row_count % col_count == col_place
    )
    local_index = jnp.where(
        holds_row,
        source_tiles // (row_count * col_count) * tile_size + pivot_sources % tile_size,
        0,
    )
    pivot_part = jnp.where(holds_row[:, None], jnp.take(slab_rows, local_index, axis=0), 0.0)
    leading = (row_place == 0) & (col_place == 0)
    initial_part = jnp.where(leading, slab_rows[:tile_size], 0.0)
    initial_top, pivot_top = lax.psum((initial_part, pivot_part), ("row", "col"))
    from_pivots = jnp.take(pivot_top, jnp.minimum(global_rows, tile_size - 1), axis=0)
    from_initial = jnp.take(initial_top, jnp.minimum(sources, tile_size - 1), axis=0)
    permuted = jnp.where(
        (global_rows < tile_size)[:, None],
        from_pivots,
        jnp.where((sources == global_rows)[:, None], slab_rows, from_initial),
    )
    highest = lax.Precision.HIGHEST
    upper_block = jnp.dot(
        lower_inv, pivot_top[:, tile_size:], precision=highest, preferred_element_type=jnp.float32
    )
    lower_panel = jnp.dot(
        permuted[:, :tile_size], upper_inv, precision=highest, preferred_element_type=jnp.float32
    )
    trailing = permuted[:, tile_size:] - jnp.dot(
        lower_panel, upper_block, precision=highest, preferred_element_type=jnp.float32
    )
    slab_out = jnp.concatenate([lower_panel, trailing], axis=1).reshape(
        1, 1, tile_rows_dev, tile_size, 2 * tile_size
    )
    return (slab_out, upper_block)


def solution(mesh):
    placed = (
        P("col", "row", None, None, None, None),
        P(),
        P("col", None, None, None),
        P(),
        P(),
        P(),
    )
    return jax.shard_map(
        per_device,
        mesh=mesh,
        in_specs=placed,
        out_specs=(P("row", "col", None, None, None), P()),
        check_vma=False,
    )
```

profile of v0, /device:TPU:0, one launch (start us, length us, event | category | flops | bytes accessed | tf_op | source)
XLA Modules:
  0.0 1934.2 jit_solution(667069928864595273)
XLA Ops:
  8.2 1.0 dynamic-slice_reduce_fusion
  9.3 0.7 reshape.322
  10.9 1.0 fusion.17
  12.0 153.8 %divide_add_fusion = f32[16,256,256]{2,1,0:T(8,128)} fusion(f32[16,256]{1,0:T(8,128)S(1)} %get-tuple-element.183, f32[16,256]{1,0:T(8,128)S(1)} %get-tuple-element.184, f32[16,256]{1,0:T(8,128)S(1)} %get-tuple-element.185, f32[16,256]{1,0:T(8,128)S(1)} %get-tuple-element.186, f32[16,256]{1,0:T(8,128)S(1)} %bitcast.101, f32[16,256]{1,0:T(8,128)S(1)} %bitcast.95, ...), kind=kLoop, calls=%fused_computation.14 | loop fusion | flops 57671680 | bytes 4456448 | tf_op jit(solution)/shard_map/add | solution.py:34
  165.8 5.3 all-to-all-start
  171.3 0.8 scatter_custom_fusion
  172.3 1.0 iota_reduce_fusion
  173.3 1534.3 %while.17 = (s32[]{:T(128)}, s32[512]{0:T(512)S(1)}, s32[512]{0:T(512)S(1)}, s32[]{:T(128)}, s32[]{:T(128)}, /*index=5*/s32[]{:T(128)}, s32[]{:T(128)}, s32[]{:T(128)}, s32[]{:T(128)}) while((s32[]{:T(128)}, s32[512]{0:T(512)S(1)}, s32[512]{0:T(512)S(1)}, s32[]{:T(128)}, s32[]{:T(128)}, /*index=5*/s32[]{:T(128)}, s32[]{:T(128)}, s32[]{:T(128)}, ...), condition=%wide.region_2.3_spmd, body=%wide.region_1.2_spmd.sunk | while | flops 20 | bytes 2363 | solution.py:51
  177.8 0.7 select_dynamic-update-slice_fusion.4
  178.6 0.7 select_dynamic-update-slice_fusion.5
  183.8 0.7 select_dynamic-update-slice_fusion.4
  184.5 0.7 select_dynamic-update-slice_fusion.5
  190.5 0.7 select_dynamic-update-slice_fusion.5
  196.5 0.7 select_dynamic-update-slice_fusion.5
  201.8 0.7 select_dynamic-update-slice_fusion.4
  207.8 0.7 select_dynamic-update-slice_fusion.4
  208.5 0.7 select_dynamic-update-slice_fusion.5
  213.8 0.7 select_dynamic-update-slice_fusion.4
  214.5 0.7 select_dynamic-update-slice_fusion.5
  219.8 0.7 select_dynamic-update-slice_fusion.4
  220.5 0.7 select_dynamic-update-slice_fusion.5
  225.8 0.7 select_dynamic-update-slice_fusion.4
  226.5 0.7 select_dynamic-update-slice_fusion.5
  231.8 0.7 select_dynamic-update-slice_fusion.4
  232.5 0.7 select_dynamic-update-slice_fusion.5
  237.8 0.7 select_dynamic-update-slice_fusion.4
  238.5 0.7 select_dynamic-update-slice_fusion.5
  243.8 0.7 select_dynamic-update-slice_fusion.4
  244.5 0.7 select_dynamic-update-slice_fusion.5
  250.5 0.7 select_dynamic-update-slice_fusion.5
  255.7 0.7 select_dynamic-update-slice_fusion.4
  261.7 0.7 select_dynamic-update-slice_fusion.4
  267.7 0.7 select_dynamic-update-slice_fusion.4
  268.4 0.7 select_dynamic-update-slice_fusion.5
  273.7 0.7 select_dynamic-update-slice_fusion.4
  274.4 0.7 select_dynamic-update-slice_fusion.5
  279.7 0.7 select_dynamic-update-slice_fusion.4
  280.4 0.7 select_dynamic-update-slice_fusion.5
  285.7 0.7 select_dynamic-update-slice_fusion.4
  286.4 0.7 select_dynamic-update-slice_fusion.5
  291.7 0.7 select_dynamic-update-slice_fusion.4
  1707.5 3.5 gather_fusion
  1711.1 5.0 gather_fusion.2
  1716.2 4.7 select_bitcast_fusion
  1720.8 5.5 copy.39
  1726.4 1.1 slice_select_fusion
  1727.4 6.2 copy.64
  1734.0 0.8 copy.65
  1734.8 5.3 copy.40
  1740.2 3.4 gather_fusion.3
  1743.6 1.0 select_select_fusion.1
  1744.6 0.9 select_reduce_fusion
  1745.5 132.6 %all-reduce.3.cloned.1.call-done = (f32[256,512]{1,0:T(8,128)}, f32[256,512]{1,0:T(8,128)}) async-done(((f32[256,512]{1,0:T(8,128)}, f32[256,512]{1,0:T(8,128)}), (f32[256,512]{1,0:T(8,128)}, f32[256,512]{1,0:T(8,128)})) %all-reduce.3.cloned.1.call-update) | async-done | bytes 1048592 | tf_op jit(solution)/shard_map/psum | solution.py:105
  1878.2 1.6 fusion.3
  1879.8 0.8 copy.45
  1880.6 8.9 gather_fusion.4
  1889.5 5.4 copy.41
  1895.0 8.9 gather_fusion.5
  1903.9 5.4 copy.43
  1909.4 6.1 fusion
  1915.5 2.0 fusion.1
  1917.5 2.0 convolution_subtract_fusion
  1919.6 2.4 pad_maximum_fusion
  1922.0 5.3 copy.46
  (1047 shorter events, 646.4 us)
Async XLA Ops:
  7.2 1908.3 %copy-start = (f32[256,256]{1,0:T(8,128)S(1)}, f32[256,256]{1,0:T(8,128)}, u32[]{:S(2)}) copy-start(f32[256,256]{1,0:T(8,128)} %param.19) | copy-start | bytes 786436
  165.8 5.4 copy-start.4
  165.8 1545.3 %all-to-all-start = ((f32[16,256,256]{2,1,0:T(8,128)}), f32[16,256,256]{2,1,0:T(8,128)}, u32[]{:S(2)}, u32[]{:S(2)}) async-start(f32[16,256,256]{2,1,0:T(8,128)} %divide_add_fusion), calls=%async_computation | async-start | bytes 8388608 | tf_op jit(solution)/shard_map/all_to_all | solution.py:75
  171.2 1707.0 %all-reduce.3.cloned.1.call-start = ((), (), s32[]{:S(2)}) async-start(), calls=%async_computation.1 | async-start | bytes 2097152 | tf_op jit(solution)/shard_map/psum | solution.py:105
  1740.2 138.0 %copy-start.3 = (f32[256,256]{1,0:T(8,128)S(1)}, f32[256,256]{1,0:T(8,128)}, u32[]{:S(2)}) copy-start(f32[256,256]{1,0:T(8,128)} %param.18) | copy-start | bytes 786436
  1878.2 2.5 copy-start.1
  1889.5 5.5 copy-start.2
Sparse Core Ops, SparseCore 0:
  1744.7 133.3 all-reduce.2
where the time goes:
time: 1950 us; the launch traced here: 1930 us
  loops' own time  867 us (44%)
  other arithmetic  542 us (28%)
  local copies, waits for them, and re-layouts  367 us (19%)
  waiting for transfers between devices  133 us (7%)
    another operation x1, loops' own time, tracked_swaps(): compact = lax.fori_loop(0, tile_size, advance, positions)  867 us
    scatter x512, other arithmetic, advance(): return compact.at[slot_here].set(at_target).at[slot_there].set(at_step)  371 us
    add x1, other arithmetic, kernel_entries(): accumulated = summand if accumulated is None else accumulated + summand  154 us
    dynamic_slice x256, local copies, waits for them, and re-layouts, advance(): slot_there = first_slot[index_now + tile_size]  148 us
    another operation x256, local copies, waits for them, and re-layouts  148 us
    psum x1, waiting for transfers between devices, per_device(): lax.psum((initial_part, pivot_part), ('row', 'col'))  133 us
  transfers between devices with their start and end apart: 2, of which 1 were waited for; matrix products, arithmetic and copies ran while one was open for 35% of the time, Pallas kernels for 0%

commit v1 on v0

--- a/solution.py
+++ b/solution.py
@@ -5,6 +5,12 @@
 
 KAPPA = 9.0
 SOFTEN = 0.05
+
+
+def meet_arrays_up(tile_in):
+    for nth in ("col", "row"):
+        tile_in = lax.psum(tile_in, axis_name=nth)
+    return tile_in
 
 
 def kernel_entries(row_points, column_points):
@@ -102,7 +108,7 @@
     pivot_part = jnp.where(holds_row[:, None], jnp.take(slab_rows, local_index, axis=0), 0.0)
     leading = (row_place == 0) & (col_place == 0)
     initial_part = jnp.where(leading, slab_rows[:tile_size], 0.0)
-    initial_top, pivot_top = lax.psum((initial_part, pivot_part), ("row", "col"))
+    initial_top, pivot_top = meet_arrays_up((initial_part, pivot_part))
     from_pivots = jnp.take(pivot_top, jnp.minimum(global_rows, tile_size - 1), axis=0)
     from_initial = jnp.take(initial_top, jnp.minimum(sources, tile_size - 1), axis=0)
     permuted = jnp.where(

time: 1950 us -> 2110 us (1.082)
  loops' own time: 867 us -> 990 us
  local copies, waits for them, and re-layouts: 367 us -> 395 us
  other arithmetic: 542 us -> 568 us
    another operation x1, loops' own time: 867 us -> 990 us  [tracked_swaps(): compact = lax.fori_loop(0, tile_size, advance, positions)]
    scatter x512, other arithmetic: 371 us -> 396 us  [advance(): return compact.at[slot_here].set(at_target).at[slot_there].set(at_step)]
    psum x1 -> x2, waiting for transfers between devices: 133 us -> 112 us  [meet_arrays_up(): tile_in = lax.psum(tile_in, axis_name=nth)]
  transfers between devices with their start and end apart: 2 -> 3, of which waited for: 1 -> 2; matrix products, arithmetic and copies ran while one was open for 35% -> 35% of each run, Pallas kernels for 0% -> 0%
where the time goes in v1:
time: 2110 us; the launch traced here: 2090 us
  loops' own time  990 us (47%)
  other arithmetic  568 us (27%)
  local copies, waits for them, and re-layouts  395 us (19%)
  waiting for transfers between devices  112 us (5%)
    another operation x1, loops' own time, tracked_swaps(): compact = lax.fori_loop(0, tile_size, advance, positions)  990 us
    scatter x512, other arithmetic, advance(): return compact.at[slot_here].set(at_target).at[slot_there].set(at_step)  396 us
    dynamic_slice x256, local copies, waits for them, and re-layouts, advance(): slot_there = first_slot[index_now + tile_size]  166 us
    another operation x256, local copies, waits for them, and re-layouts  158 us
    add x1, other arithmetic, kernel_entries(): accumulated = summand if accumulated is None else accumulated + summand  154 us
    psum x2, waiting for transfers between devices, meet_arrays_up(): tile_in = lax.psum(tile_in, axis_name=nth)  112 us
  transfers between devices with their start and end apart: 3, of which 2 were waited for; matrix products, arithmetic and copies ran while one was open for 35% of the time, Pallas kernels for 0%

profile of v1, /device:TPU:0, one launch (start us, length us, event | category | flops | bytes accessed | tf_op | source)
XLA Modules:
  0.0 2090.7 jit_solution(8806377221871084311)
XLA Ops:
  8.2 1.0 dynamic-slice_reduce_fusion
  10.9 1.0 fusion.17
  12.0 153.9 %divide_add_fusion = f32[16,256,256]{2,1,0:T(8,128)} fusion(f32[16,256]{1,0:T(8,128)S(1)} %get-tuple-element.185, f32[16,256]{1,0:T(8,128)S(1)} %get-tuple-element.186, f32[16,256]{1,0:T(8,128)S(1)} %get-tuple-element.187, f32[16,256]{1,0:T(8,128)S(1)} %get-tuple-element.188, f32[16,256]{1,0:T(8,128)S(1)} %bitcast.101, f32[16,256]{1,0:T(8,128)S(1)} %bitcast.95, ...), kind=kLoop, calls=%fused_computation.14 | loop fusion | flops 57671680 | bytes 4456448 | tf_op jit(solution)/shard_map/add | solution.py:40
  165.9 5.3 all-to-all-start
  171.4 0.8 scatter_custom_fusion
  172.3 1.0 iota_reduce_fusion
  173.3 1710.4 %while.17 = (s32[]{:T(128)}, s32[512]{0:T(512)S(1)}, s32[512]{0:T(512)S(1)}, s32[]{:T(128)}, s32[]{:T(128)}, /*index=5*/s32[]{:T(128)}, s32[]{:T(128)}, s32[]{:T(128)}, s32[]{:T(128)}) while((s32[]{:T(128)}, s32[512]{0:T(512)S(1)}, s32[512]{0:T(512)S(1)}, s32[]{:T(128)}, s32[]{:T(128)}, /*index=5*/s32[]{:T(128)}, s32[]{:T(128)}, s32[]{:T(128)}, ...), condition=%wide.region_2.3_spmd, body=%wide.region_1.2_spmd.sunk | while | flops 20 | bytes 2363 | solution.py:57
  178.5 0.8 select_dynamic-update-slice_fusion.4
  198.5 0.8 select_dynamic-update-slice_fusion.4
  226.0 0.8 select_dynamic-update-slice_fusion.5
  246.1 0.8 select_dynamic-update-slice_fusion.5
  252.0 0.8 select_dynamic-update-slice_fusion.4
  272.0 0.8 select_dynamic-update-slice_fusion.4
  279.5 0.8 select_dynamic-update-slice_fusion.5
  299.5 0.8 select_dynamic-update-slice_fusion.5
  305.4 0.8 select_dynamic-update-slice_fusion.4
  325.5 0.8 select_dynamic-update-slice_fusion.4
  353.0 0.8 select_dynamic-update-slice_fusion.5
  373.0 0.8 select_dynamic-update-slice_fusion.5
  378.9 0.8 select_dynamic-update-slice_fusion.4
  399.0 0.8 select_dynamic-update-slice_fusion.4
  406.4 0.8 select_dynamic-update-slice_fusion.5
  426.5 0.8 select_dynamic-update-slice_fusion.5
  432.4 0.8 select_dynamic-update-slice_fusion.4
  452.4 0.8 select_dynamic-update-slice_fusion.4
  479.9 0.8 select_dynamic-update-slice_fusion.5
  499.9 0.8 select_dynamic-update-slice_fusion.5
  505.8 0.8 select_dynamic-update-slice_fusion.4
  525.9 0.8 select_dynamic-update-slice_fusion.4
  533.3 0.8 select_dynamic-update-slice_fusion.5
  553.4 0.8 select_dynamic-update-slice_fusion.5
  559.3 0.8 select_dynamic-update-slice_fusion.4
  579.3 0.8 select_dynamic-update-slice_fusion.4
  606.8 0.8 select_dynamic-update-slice_fusion.5
  626.9 0.8 select_dynamic-update-slice_fusion.5
  632.8 0.8 select_dynamic-update-slice_fusion.4
  652.8 0.8 select_dynamic-update-slice_fusion.4
  660.3 0.8 select_dynamic-update-slice_fusion.5
  680.3 0.8 select_dynamic-update-slice_fusion.5
  686.2 0.8 select_dynamic-update-slice_fusion.4
  1883.7 3.5 gather_fusion
  1887.3 5.0 gather_fusion.2
  1892.3 4.7 select_bitcast_fusion
  1897.0 5.5 copy.39
  1902.5 1.1 slice_select_fusion
  1903.6 6.2 copy.64
  1910.1 0.9 copy.65
  1911.0 5.3 copy.40
  1916.4 3.4 gather_fusion.3
  1919.8 0.9 select_select_fusion.1
  1921.1 54.1 %all-reduce.7.cloned.1.call-done = (f32[256,512]{1,0:T(8,128)}, f32[256,512]{1,0:T(8,128)}) async-done(((f32[256,512]{1,0:T(8,128)}, f32[256,512]{1,0:T(8,128)}), (f32[256,512]{1,0:T(8,128)}, f32[256,512]{1,0:T(8,128)})) %all-reduce.7.cloned.1.call-update) | async-done | bytes 1048592 | tf_op jit(solution)/shard_map/psum | solution.py:12
  1975.3 0.9 select_reduce_fusion
  1976.2 58.3 %all-reduce.5.cloned.1.call-done = (f32[256,512]{1,0:T(8,128)}, f32[256,512]{1,0:T(8,128)}) async-done(((f32[256,512]{1,0:T(8,128)}, f32[256,512]{1,0:T(8,128)}), (f32[256,512]{1,0:T(8,128)}, f32[256,512]{1,0:T(8,128)})) %all-reduce.5.cloned.1.call-update) | async-done | bytes 1048592 | tf_op jit(solution)/shard_map/psum | solution.py:12
  2034.6 1.6 fusion.3
  2036.2 0.8 copy.45
  2037.0 9.0 gather_fusion.4
  2046.0 5.5 copy.41
  2051.5 8.9 gather_fusion.5
  2060.4 5.5 copy.43
  2065.8 6.1 fusion
  2072.0 2.1 fusion.1
  2074.0 2.1 convolution_subtract_fusion
  2076.1 2.4 pad_maximum_fusion
  2078.5 5.3 copy.46
  (1050 shorter events, 698.7 us)
Async XLA Ops:
  7.2 2064.8 %copy-start = (f32[256,256]{1,0:T(8,128)S(1)}, f32[256,256]{1,0:T(8,128)}, u32[]{:S(2)}) copy-start(f32[256,256]{1,0:T(8,128)} %param.19) | copy-start | bytes 786436
  165.9 5.4 copy-start.4
  165.9 1721.4 %all-to-all-start = ((f32[16,256,256]{2,1,0:T(8,128)}), f32[16,256,256]{2,1,0:T(8,128)}, u32[]{:S(2)}, u32[]{:S(2)}) async-start(f32[16,256,256]{2,1,0:T(8,128)} %divide_add_fusion), calls=%async_computation | async-start | bytes 8388608 | tf_op jit(solution)/shard_map/all_to_all | solution.py:81
  171.2 1804.0 %all-reduce.7.cloned.1.call-start = ((), (), s32[]{:S(2)}) async-start(), calls=%async_computation.2 | async-start | bytes 2097152 | tf_op jit(solution)/shard_map/psum | solution.py:12
  1916.4 118.2 %copy-start.3 = (f32[256,256]{1,0:T(8,128)S(1)}, f32[256,256]{1,0:T(8,128)}, u32[]{:S(2)}) copy-start(f32[256,256]{1,0:T(8,128)} %param.18) | copy-start | bytes 786436
  1920.8 113.8 %all-reduce.5.cloned.1.call-start = ((), (), s32[]{:S(2)}) async-start(), calls=%async_computation.1 | async-start | bytes 2097152 | tf_op jit(solution)/shard_map/psum | solution.py:12
  2034.5 2.5 copy-start.1
  2046.0 5.5 copy-start.2
Sparse Core Ops, SparseCore 0:
  1920.9 54.3 all-reduce.6
  1978.5 56.0 all-reduce.4
